TPU v7x, 128 devices: a whole 4x4x4 slice. The times are simulated.
128 devices in a mesh: row: 8 (over y_hi, x), col: 16 (over z, y_lo, core).
Axes of the slice: x: 4, y: 4 (y_hi: 2, y_lo: 2; y = y_hi * 2 + y_lo), z: 4, core: 2. Of those that a mesh axis runs over, the one named last changes fastest.
Arguments:
- features: bfloat16 [64, 1024, 1024], P(None, 'col', 'row'), may hold values from -120 to 120
- conv_first: bfloat16 [9, 64, 64], replicated, may hold values from -0.25 to 0.25
- conv_second: bfloat16 [9, 64, 64], replicated, may hold values from -0.25 to 0.25
- head_weight: bfloat16 [37, 64], replicated, may hold values from -0.75 to 0.75
- head_bias: float32 [37], replicated, may hold values from -4 to 4
- cotangent: bfloat16 [37, 1024, 1024], P(None, 'col', 'row'), may hold values from -6 to 6
Outputs:
- logits: bfloat16 [37, 1024, 1024], P(None, 'col', 'row')
- input_grad: bfloat16 [64, 1024, 1024], P(None, 'col', 'row')
- grad_first: float32 [9, 64, 64], replicated
- grad_second: float32 [9, 64, 64], replicated
- grad_head: float32 [37, 64], replicated
- grad_bias: float32 [37], replicated
All inputs are finite; a program needn't handle non-finite values.
Results may differ from a plain program's by a relative error of at most 0.007.
Values may be sent and summed in bfloat16 or wider, within the bound.
No kernel may reach another device: no remote copies, remote signals or barrier semaphores. Data moves between devices by JAX's collectives and lax.ppermute only.
A program may use at most 128 MiB of HBM per device.

v0:
```python
import jax
import jax.numpy as jnp
from jax import lax
from jax.sharding import PartitionSpec as P

DILATION_STEP = 16
epsilon = 1e-05


def with_halo(block, sides, width):
    for axis, dim in sides:
        count = lax.axis_size(axis)
        forward = [(i, i + 1) for i in range(count - 1)]
        backward = [(target, source) for source, target in forward]
        low = lax.ppermute(
            lax.slice_in_dim(block, block.shape[dim] - width, None, axis=dim), axis, forward
        )
        high = lax.ppermute(lax.slice_in_dim(block, 0, width, axis=dim), axis, backward)
        block = jnp.concatenate([low, block, high], axis=dim)
    return block


def as_sent(shard):

    def short(part):
        return part.astype(jnp.bfloat16) if part.dtype == jnp.float32 else part

    return jax.tree.map(short, shard)


def elu_apply(value_entries):
    return jnp.where(
        value_entries > 0, value_entries, jnp.exp(jnp.minimum(value_entries, 0.0)) - 1.0
    )


def elu_slope(value_entries):
    return jnp.where(value_entries > 0, 1.0, jnp.exp(jnp.minimum(value_entries, 0.0)))


def widen(value_entries):
    return with_halo(value_entries, (("row", 2), ("col", 1)), DILATION_STEP)


def widen_grad(value_entries):
    return with_halo(value_entries, (("row", 2), ("col", 1)), DILATION_STEP)


def tap_window(padded, kernel_row, kernel_column, adjoint, col_count, row_count):
    shift_direction = -1 if adjoint else 1
    column_shift = DILATION_STEP + shift_direction * DILATION_STEP * (kernel_column - 1)
    row_shift = DILATION_STEP + shift_direction * DILATION_STEP * (kernel_row - 1)
    window = padded[:, column_shift : column_shift + col_count, row_shift : row_shift + row_count]
    return window.reshape(padded.shape[0], col_count * row_count)


def convolve(padded, weights, col_count, row_count, adjoint):
    running = jnp.zeros((weights.shape[1], col_count * row_count), jnp.float32)
    for kernel_row in range(3):
        for kernel_column in range(3):
            window = tap_window(padded, kernel_row, kernel_column, adjoint, col_count, row_count)
            matrix = weights[3 * kernel_row + kernel_column]
            if adjoint:
                matrix = matrix.T
            running = running + jnp.dot(matrix, window, preferred_element_type=jnp.float32)
    return running.reshape(-1, col_count, row_count)


def weight_terms(gradient, padded, col_count, row_count):
    flattened = gradient.reshape(gradient.shape[0], -1)
    collected = []
    for kernel_row in range(3):
        for kernel_column in range(3):
            window = tap_window(padded, kernel_row, kernel_column, False, col_count, row_count)
            collected.append(
                lax.dot_general(
                    flattened, window, (((1,), (1,)), ((), ())), preferred_element_type=jnp.float32
                )
            )
    return jnp.stack(collected, 0)


def normalize(activation, cell_count):
    totals = lax.psum(jnp.sum(activation, axis=(1, 2)), ("row", "col"))
    average = totals / cell_count
    centered = activation - average[:, None, None]
    spread = lax.psum(jnp.sum(centered * centered, axis=(1, 2)), ("row", "col")) / cell_count
    inverse_std = lax.rsqrt(spread + epsilon)
    return (centered * inverse_std[:, None, None], inverse_std)


def norm_back(gradient, normed, inverse_std, cell_count):
    first_sum, second_sum = lax.psum(
        (jnp.sum(gradient, axis=(1, 2)), jnp.sum(gradient * normed, axis=(1, 2))), ("row", "col")
    )
    first_mean = first_sum / cell_count
    second_mean = second_sum / cell_count
    return inverse_std[:, None, None] * (
        gradient - first_mean[:, None, None] - normed * second_mean[:, None, None]
    )


def mirror_prepare(tensor, col_devices):
    planes, col_count, row_count = tensor.shape
    slab_rows = row_count // col_devices
    shaped = tensor.reshape(planes, col_count, col_devices, slab_rows).transpose(2, 1, 0, 3)
    return shaped.reshape(col_devices, col_count, planes * slab_rows)


def mirror_middle(received):
    return received.reshape(received.shape[1], 1, received.shape[2])


def mirror_tail(received, col_devices, row_devices):
    return received.reshape(received.shape[0], col_devices, row_devices, received.shape[2])


def mirror_finish(received, planes, row_devices):
    row_count = received.shape[0]
    slab_rows = received.shape[3] // planes
    shaped = received.reshape(row_count, row_devices, planes, slab_rows).transpose(2, 1, 3, 0)
    return shaped.reshape(planes, row_devices * slab_rows, row_count)


def mirror_half(tensors):
    col_devices = lax.axis_size("col")
    row_devices = lax.axis_size("row")
    planes = tuple((member.shape[0] for member in tensors))
    first = lax.all_to_all(
        as_sent(tuple((mirror_prepare(member, col_devices) for member in tensors))),
        "col",
        split_axis=0,
        concat_axis=1,
        tiled=True,
    )
    second = lax.all_to_all(
        as_sent(tuple((mirror_middle(member) for member in first))),
        ("row", "col"),
        split_axis=0,
        concat_axis=1,
        tiled=True,
    )
    third = lax.all_to_all(
        as_sent(tuple((mirror_tail(member, col_devices, row_devices) for member in second))),
        "col",
        split_axis=1,
        concat_axis=0,
        tiled=True,
    )
    return tuple(
        (
            mirror_finish(member, count_planes, row_devices)
            for member, count_planes in zip(third, planes)
        )
    )


def mirror_full(tensors):
    col_devices = lax.axis_size("col")
    row_devices = lax.axis_size("row")
    planes = tuple((member.shape[0] for member in tensors))
    first = lax.all_to_all(
        tuple((mirror_prepare(member, col_devices) for member in tensors)),
        "col",
        split_axis=0,
        concat_axis=1,
        tiled=True,
    )
    second = lax.all_to_all(
        tuple((mirror_middle(member) for member in first)),
        ("row", "col"),
        split_axis=0,
        concat_axis=1,
        tiled=True,
    )
    third = lax.all_to_all(
        tuple((mirror_tail(member, col_devices, row_devices) for member in second)),
        "col",
        split_axis=1,
        concat_axis=0,
        tiled=True,
    )
    return tuple(
        (
            mirror_finish(member, count_planes, row_devices)
            for member, count_planes in zip(third, planes)
        )
    )


def on_device(features, conv_first, conv_second, head_weight, head_bias, cotangent):
    channels, col_count, row_count = features.shape
    length = col_count * lax.axis_size("col")
    cell_count = float(length * length)
    cot_mirror = mirror_half((cotangent,))[0]
    wide_in = widen(features)
    act_first = convolve(wide_in, conv_first, col_count, row_count, False)
    normed_first, inverse_first = normalize(act_first, cell_count)
    hidden_first = elu_apply(normed_first).astype(jnp.bfloat16)
    wide_hidden = widen(hidden_first)
    act_second = convolve(wide_hidden, conv_second, col_count, row_count, False)
    normed_second, inverse_second = normalize(act_second, cell_count)
    summed = normed_second + features.astype(jnp.float32)
    hidden = elu_apply(summed).astype(jnp.bfloat16)
    flat_hidden = hidden.reshape(channels, -1)
    raw_logits = (
        jnp.dot(head_weight, flat_hidden, preferred_element_type=jnp.float32) + head_bias[:, None]
    ).reshape(-1, col_count, row_count)
    logit_mirror = mirror_full((raw_logits,))[0]
    logits = (0.5 * (raw_logits + logit_mirror)).astype(jnp.bfloat16)
    grad_sym = (0.5 * (cotangent.astype(jnp.float32) + cot_mirror.astype(jnp.float32))).astype(
        jnp.bfloat16
    )
    flat_sym = grad_sym.reshape(grad_sym.shape[0], -1)
    bias_term = jnp.sum(flat_sym, axis=1, dtype=jnp.float32)
    head_term = lax.dot_general(
        flat_sym, flat_hidden, (((1,), (1,)), ((), ())), preferred_element_type=jnp.float32
    )
    grad_hidden = jnp.dot(head_weight.T, flat_sym, preferred_element_type=jnp.float32).reshape(
        channels, col_count, row_count
    )
    grad_summed = grad_hidden * elu_slope(summed)
    grad_act_second = norm_back(grad_summed, normed_second, inverse_second, cell_count).astype(
        jnp.bfloat16
    )
    second_term = weight_terms(grad_act_second, wide_hidden, col_count, row_count)
    grad_hidden_first = convolve(
        widen_grad(grad_act_second), conv_second, col_count, row_count, True
    )
    grad_normed_first = grad_hidden_first * elu_slope(normed_first)
    grad_act_first = norm_back(grad_normed_first, normed_first, inverse_first, cell_count).astype(
        jnp.bfloat16
    )
    first_term = weight_terms(grad_act_first, wide_in, col_count, row_count)
    input_grad = (
        convolve(widen_grad(grad_act_first), conv_first, col_count, row_count, True) + grad_summed
    ).astype(jnp.bfloat16)
    reduced = lax.psum((first_term, second_term, head_term, bias_term), ("row", "col"))
    inverse_len = 1.0 / length
    return (
        logits,
        input_grad,
        reduced[0] * inverse_len,
        reduced[1] * inverse_len,
        reduced[2] * inverse_len,
        reduced[3] * inverse_len,
    )


def solution(mesh):
    placed = (P(None, "col", "row"), P(), P(), P(), P(), P(None, "col", "row"))
    return jax.shard_map(
        on_device,
        mesh=mesh,
        in_specs=placed,
        out_specs=(P(None, "col", "row"), P(None, "col", "row"), P(), P(), P(), P()),
        check_vma=False,
    )
```

profile of v0, /device:TPU:1, one launch (start us, length us, event | category | flops | bytes accessed | tf_op | source)
XLA Modules:
  0.0 945.5 jit_solution(8504347659862040630)
XLA Ops:
  12.6 5.3 collective-permute-start
  21.0 7.8 all-to-all-start.3
  45.4 7.2 collective-permute-done.3
  63.5 67.2 %psum.84 = f32[64]{0:T(128)S(1)} all-reduce(f32[64]{0:T(128)S(1)} %get-tuple-element.108), channel_id=1, replica_groups=mesh['row'=8,'col'=16] {'row','col'}, use_global_device_ids=true, to_apply=%region_1.0 | all-reduce | flops 64 | bytes 512 | tf_op jit(solution)/shard_map/psum | solution.py:84
  131.1 63.5 %psum.85 = f32[64]{0:T(128)S(1)} all-reduce(f32[64]{0:T(128)S(1)} %multiply_reduce_fusion.2), channel_id=1, replica_groups=mesh['row'=8,'col'=16] {'row','col'}, use_global_device_ids=true, to_apply=%region_3.0 | all-reduce | flops 64 | bytes 512 | tf_op jit(solution)/shard_map/psum | solution.py:87
  209.8 4.3 collective-permute-done.5
  233.1 11.2 %all-to-all-start.4 = ((bf16[128,2,1184]{2,1,0:T(2,128)(2,1)}), bf16[128,2,1184]{2,1,0:T(2,128)(2,1)}, u32[]{:S(2)}, u32[]{:S(2)}) async-start(bf16[128,2,1184]{2,1,0:T(2,128)(2,1)} %reshape.289), calls=%async_computation.4 | async-start | bytes 1310720 | tf_op jit(solution)/shard_map/all_to_all | solution.py:136
  247.3 4.2 pad_maximum_fusion.1
  260.6 67.2 %psum.86 = f32[64]{0:T(128)S(1)} all-reduce(f32[64]{0:T(128)S(1)} %get-tuple-element.110), channel_id=1, replica_groups=mesh['row'=8,'col'=16] {'row','col'}, use_global_device_ids=true, to_apply=%region_5.6 | all-reduce | flops 64 | bytes 512 | tf_op jit(solution)/shard_map/psum | solution.py:84
  327.7 6.2 reshape.290
  336.5 4.3 all-to-all-start.5
  342.8 65.3 %psum.87 = f32[64]{0:T(128)S(1)} all-reduce(f32[64]{0:T(128)S(1)} %fusion.19), channel_id=1, replica_groups=mesh['row'=8,'col'=16] {'row','col'}, use_global_device_ids=true, to_apply=%region_7.8 | all-reduce | flops 64 | bytes 512 | tf_op jit(solution)/shard_map/psum | solution.py:87
  409.4 12.2 %reshape.288 = f32[128,8,37,8]{3,2,1,0:T(8,128)} reshape(f32[16,8,1,8,296]{4,3,1,0,2:T(8,128)} %convert_bitcast_fusion) | data formatting | bytes 2424832 | tf_op jit(solution)/shard_map/convert_element_type | solution.py:211
  421.5 11.1 %copy.273 = f32[37,8,8,128]{3,2,1,0:T(8,128)S(1)} copy(f32[37,8,8,128]{2,0,1,3:T(8,128)} %bitcast.528) | data formatting | bytes 2424832 | tf_op jit(solution)/shard_map/convert_element_type | solution.py:211
  439.4 62.9 %all-reduce.1 = (f32[64]{0:T(128)S(1)}, f32[64]{0:T(128)S(1)}) all-reduce(f32[64]{0:T(128)S(1)} %get-tuple-element.39, f32[64]{0:T(128)S(1)} %get-tuple-element.38), channel_id=1, replica_groups=mesh['row'=8,'col'=16] {'row','col'}, use_global_device_ids=true, to_apply=%region_11.12 | all-reduce | flops 128 | bytes 1024 | tf_op jit(solution)/shard_map/psum | solution.py:93
  524.1 4.7 collective-permute-start.8
  538.7 5.1 copy.259
  546.9 5.3 all-to-all-start
  568.5 8.1 collective-permute-done.11
  576.5 7.2 collective-permute-done.10
  595.0 67.2 %all-reduce = (f32[64]{0:T(128)S(1)}, f32[64]{0:T(128)S(1)}, f32[37,64]{1,0:T(8,128)S(1)}, f32[37]{0:T(128)S(1)}) all-reduce(f32[64]{0:T(128)S(1)} %get-tuple-element.37, f32[64]{0:T(128)S(1)} %get-tuple-element.36, f32[37,64]{1,0:T(8,128)S(1)} %convolution_bitcast_fusion.23, ...), channel_id=1, replica_groups=mesh['row'=8,'col'=16] {'row','col'}, use_global_device_ids=true, to_apply=%region_15.16 | all-reduce | flops 2533 | bytes 20264 | tf_op jit(solution)/shard_map/psum | solution.py:93
  680.8 5.1 collective-permute-start.12
  699.2 4.6 collective-permute-start.15
  708.2 125.5 %all-reduce.5.cloned.1.call-done = (f32[9,64,64]{2,1,0:T(8,128)}, f32[9,64,64]{2,1,0:T(8,128)}) async-done(((f32[9,64,64]{2,1,0:T(8,128)}, f32[9,64,64]{2,1,0:T(8,128)}), (f32[9,64,64]{2,1,0:T(8,128)}, f32[9,64,64]{2,1,0:T(8,128)})) %all-reduce.5.cloned.1.call-update) | async-done | bytes 294928 | tf_op jit(solution)/shard_map/psum | solution.py:238
  837.1 4.8 maximum_maximum_fusion.3
  848.5 4.2 copy.261
  852.7 7.4 all-to-all-start.1
  866.1 17.9 %all-to-all-done.1 = f32[1024,1,296]{2,1,0:T(1,128)} async-done(((f32[1024,1,296]{2,1,0:T(1,128)}), f32[1024,1,296]{2,1,0:T(1,128)}, u32[]{:S(2)}, u32[]{:S(2)}) %all-to-all-start.1) | async-done | bytes 1212448 | tf_op jit(solution)/shard_map/all_to_all | solution.py:169
  887.0 5.5 all-to-all-start.2
  898.6 15.5 %all-to-all-done.2 = f32[8,16,8,296]{3,2,0,1:T(8,128)} async-done(((f32[8,16,8,296]{3,2,0,1:T(8,128)}), f32[8,16,8,296]{3,2,0,1:T(8,128)}, u32[]{:S(2)}, u32[]{:S(2)}) %all-to-all-start.2) | async-done | bytes 1212448 | tf_op jit(solution)/shard_map/all_to_all | solution.py:176
  914.1 12.2 %reshape.287 = f32[128,8,37,8]{3,2,1,0:T(8,128)} reshape(f32[16,8,1,8,296]{4,3,1,0,2:T(8,128)} %bitcast.32) | data formatting | bytes 2424832 | tf_op jit(solution)/shard_map/reshape | solution.py:121
  926.2 11.2 %copy.265 = f32[37,8,8,128]{3,2,1,0:T(8,128)S(1)} copy(f32[37,8,8,128]{2,0,1,3:T(8,128)} %bitcast.529) | data formatting | bytes 2424832 | tf_op jit(solution)/shard_map/transpose | solution.py:121
  (261 shorter events, 219.1 us)
Async XLA Ops:
  7.2 427.7 %copy-start = (bf16[37,64]{1,0:T(8,128)(2,1)S(1)}, bf16[37,64]{1,0:T(8,128)(2,1)}, u32[]{:S(2)}) copy-start(bf16[37,64]{1,0:T(8,128)(2,1)} %param.9) | copy-start | bytes 14212
  10.3 22.0 %collective-permute-start.1 = (bf16[64,64,16]{1,2,0:T(8,128)(2,1)}, bf16[64,64,16]{1,2,0:T(8,128)(2,1)}, u32[]{:S(2)}, u32[]{:S(2)}) collective-permute-start(bf16[64,64,16]{1,2,0:T(8,128)(2,1)} %copy.320), channel_id=1, source_target_pairs={{16,0},{32,16},{48,32},{64,48},{80,64},{96,80},{112,96},{17,1},{33... | collective-permute-start | bytes 393224 | tf_op jit(solution)/shard_map/ppermute | solution.py:18
  12.6 16.9 %collective-permute-start = (bf16[64,64,16]{1,2,0:T(8,128)(2,1)}, bf16[64,64,16]{1,2,0:T(8,128)(2,1)}, u32[]{:S(2)}, u32[]{:S(2)}) collective-permute-start(bf16[64,64,16]{1,2,0:T(8,128)(2,1)} %copy.319), channel_id=1, source_target_pairs={{0,16},{16,32},{32,48},{48,64},{64,80},{80,96},{96,112},{1,17},{17... | collective-permute-start | bytes 393224 | tf_op jit(solution)/shard_map/ppermute | solution.py:15
  21.0 205.0 %all-to-all-start.3 = ((bf16[16,64,296]{2,1,0:T(8,128)(2,1)}), bf16[16,64,296]{2,1,0:T(8,128)(2,1)}, u32[]{:S(2)}, u32[]{:S(2)}) async-start(bf16[16,64,296]{2,1,0:T(8,128)(2,1)} %copy.268), calls=%async_computation.3 | async-start | bytes 1572864 | tf_op jit(solution)/shard_map/all_to_all | solution.py:129
  29.6 23.1 %copy-start.4 = (bf16[64,64,128]{2,0,1:T(8,128)(2,1)}, bf16[64,64,128]{2,0,1:T(8,128)(2,1)S(1)}, u32[]{:S(2)}) copy-start(bf16[64,64,128]{2,0,1:T(8,128)(2,1)S(1)} %copy.226) | copy-start | bytes 3145732
  32.3 20.3 %copy-start.9 = (bf16[64,64,16]{2,0,1:T(8,128)(2,1)}, bf16[64,64,16]{2,0,1:T(8,128)(2,1)S(1)}, u32[]{:S(2)}) copy-start(bf16[64,64,16]{2,0,1:T(8,128)(2,1)S(1)} %copy.225) | copy-start | bytes 393220
  35.1 17.6 %copy-start.7 = (bf16[64,64,16]{2,0,1:T(8,128)(2,1)}, bf16[64,64,16]{2,0,1:T(8,128)(2,1)S(1)}, u32[]{:S(2)}) copy-start(bf16[64,64,16]{2,0,1:T(8,128)(2,1)S(1)} %copy.227) | copy-start | bytes 393220
  35.7 9.7 %collective-permute-start.2 = (bf16[64,16,160]{2,0,1:T(8,128)(2,1)S(1)}, bf16[64,16,160]{2,0,1:T(8,128)(2,1)S(1)}, u32[]{:S(2)}, u32[]{:S(2)}) collective-permute-start(bf16[64,16,160]{2,0,1:T(8,128)(2,1)S(1)} %get-tuple-element.66), channel_id=1, source_target_pairs={{0,1},{1,2},{2,3},{3,4},{4,5},{5,6},{6,7},{7,8},{8,9},{9,10},{10,1... | collective-permute-start | bytes 983048 | tf_op jit(solution)/shard_map/ppermute | solution.py:15
  39.3 13.3 %collective-permute-start.3 = (bf16[64,16,160]{2,0,1:T(8,128)(2,1)S(1)}, bf16[64,16,160]{2,0,1:T(8,128)(2,1)S(1)}, u32[]{:S(2)}, u32[]{:S(2)}) collective-permute-start(bf16[64,16,160]{2,0,1:T(8,128)(2,1)S(1)} %get-tuple-element.67), channel_id=1, source_target_pairs={{1,0},{2,1},{3,2},{4,3},{5,4},{6,5},{7,6},{8,7},{9,8},{10,9},{11,1... | collective-permute-start | bytes 983048 | tf_op jit(solution)/shard_map/ppermute | solution.py:18
  195.2 52.0 %copy-start.2 = (bf16[64,64,128]{2,0,1:T(8,128)(2,1)}, bf16[64,64,128]{2,0,1:T(8,128)(2,1)S(1)}, u32[]{:S(2)}) copy-start(bf16[64,64,128]{2,0,1:T(8,128)(2,1)S(1)} %fusion.5) | copy-start | bytes 3145732
  199.3 7.2 collective-permute-start.4
  205.2 8.9 collective-permute-start.5
  220.2 27.0 %collective-permute-start.7 = (bf16[64,16,160]{2,0,1:T(8,128)(2,1)}, bf16[64,16,160]{2,0,1:T(8,128)(2,1)}, u32[]{:S(2)}, u32[]{:S(2)}) collective-permute-start(bf16[64,16,160]{2,0,1:T(8,128)(2,1)} %get-tuple-element.62), channel_id=1, source_target_pairs={{1,0},{2,1},{3,2},{4,3},{5,4},{6,5},{7,6},{8,7},{9,8},{10,9},{11,1... | collective-permute-start | bytes 983048 | tf_op jit(solution)/shard_map/ppermute | solution.py:18
  224.1 23.1 %collective-permute-start.6 = (bf16[64,16,160]{2,0,1:T(8,128)(2,1)}, bf16[64,16,160]{2,0,1:T(8,128)(2,1)}, u32[]{:S(2)}, u32[]{:S(2)}) collective-permute-start(bf16[64,16,160]{2,0,1:T(8,128)(2,1)} %get-tuple-element.63), channel_id=1, source_target_pairs={{0,1},{1,2},{2,3},{3,4},{4,5},{5,6},{6,7},{7,8},{8,9},{9,10},{10,1... | collective-permute-start | bytes 983048 | tf_op jit(solution)/shard_map/ppermute | solution.py:15
  233.1 94.7 %all-to-all-start.4 = ((bf16[128,2,1184]{2,1,0:T(2,128)(2,1)}), bf16[128,2,1184]{2,1,0:T(2,128)(2,1)}, u32[]{:S(2)}, u32[]{:S(2)}) async-start(bf16[128,2,1184]{2,1,0:T(2,128)(2,1)} %reshape.289), calls=%async_computation.4 | async-start | bytes 1310720 | tf_op jit(solution)/shard_map/all_to_all | solution.py:136
  336.5 71.6 %all-to-all-start.5 = ((bf16[8,16,8,296]{3,2,0,1:T(8,128)(2,1)}), bf16[8,16,8,296]{3,2,0,1:T(8,128)(2,1)S(1)}, u32[]{:S(2)}, u32[]{:S(2)}) async-start(bf16[8,16,8,296]{3,2,0,1:T(8,128)(2,1)} %copy.271), calls=%async_computation.5 | async-start | bytes 1572864 | tf_op jit(solution)/shard_map/all_to_all | solution.py:143
  517.0 11.8 %copy-start.48 = (f32[37]{0:T(128)S(1)}, f32[37]{0:T(128)}, u32[]{:S(2)}) copy-start(f32[37]{0:T(128)} %param.10) | copy-start | bytes 448
  522.8 33.1 %collective-permute-start.9 = (bf16[64,64,16]{1,2,0:T(8,128)(2,1)}, bf16[64,64,16]{1,2,0:T(8,128)(2,1)}, u32[]{:S(2)}, u32[]{:S(2)}) collective-permute-start(bf16[64,64,16]{1,2,0:T(8,128)(2,1)} %copy.276), channel_id=1, source_target_pairs={{16,0},{32,16},{48,32},{64,48},{80,64},{96,80},{112,96},{17,1},{33... | collective-permute-start | bytes 393224 | tf_op jit(solution)/shard_map/ppermute | solution.py:18
  524.1 28.4 %collective-permute-start.8 = (bf16[64,64,16]{1,2,0:T(8,128)(2,1)}, bf16[64,64,16]{1,2,0:T(8,128)(2,1)}, u32[]{:S(2)}, u32[]{:S(2)}) collective-permute-start(bf16[64,64,16]{1,2,0:T(8,128)(2,1)} %copy.275), channel_id=1, source_target_pairs={{0,16},{16,32},{32,48},{48,64},{64,80},{80,96},{96,112},{1,17},{17... | collective-permute-start | bytes 393224 | tf_op jit(solution)/shard_map/ppermute | solution.py:15
  546.9 301.6 %all-to-all-start = ((f32[16,64,296]{2,1,0:T(8,128)}), f32[16,64,296]{2,1,0:T(8,128)}, u32[]{:S(2)}, u32[]{:S(2)}) async-start(f32[16,64,296]{2,1,0:T(8,128)} %copy.260), calls=%async_computation | async-start | bytes 3145728 | tf_op jit(solution)/shard_map/all_to_all | solution.py:162
  552.3 281.4 %all-reduce.5.cloned.1.call-start = ((), (), s32[]{:S(2)}) async-start(), calls=%async_computation.6 | async-start | bytes 1179648 | tf_op jit(solution)/shard_map/psum | solution.py:238
  561.2 15.3 %collective-permute-start.11 = (bf16[64,16,160]{2,0,1:T(8,128)(2,1)S(1)}, bf16[64,16,160]{2,0,1:T(8,128)(2,1)S(1)}, u32[]{:S(2)}, u32[]{:S(2)}) collective-permute-start(bf16[64,16,160]{2,0,1:T(8,128)(2,1)S(1)} %get-tuple-element.58), channel_id=1, source_target_pairs={{0,1},{1,2},{2,3},{3,4},{4,5},{5,6},{6,7},{7,8},{8,9},{9,10},{10,1... | collective-permute-start | bytes 983048 | tf_op jit(solution)/shard_map/ppermute | solution.py:15
  564.8 18.9 %collective-permute-start.10 = (bf16[64,16,160]{2,0,1:T(8,128)(2,1)S(1)}, bf16[64,16,160]{2,0,1:T(8,128)(2,1)S(1)}, u32[]{:S(2)}, u32[]{:S(2)}) collective-permute-start(bf16[64,16,160]{2,0,1:T(8,128)(2,1)S(1)} %get-tuple-element.59), channel_id=1, source_target_pairs={{1,0},{2,1},{3,2},{4,3},{5,4},{6,5},{7,6},{8,7},{9,8},{10,9},{11,1... | collective-permute-start | bytes 983048 | tf_op jit(solution)/shard_map/ppermute | solution.py:18
  673.5 12.3 %copy-start.47 = (f32[9,64,64]{2,1,0:T(8,128)}, f32[9,64,64]{2,1,0:T(8,128)S(1)}, u32[]{:S(2)}) copy-start(f32[9,64,64]{2,1,0:T(8,128)S(1)} %fusion.34) | copy-start | bytes 442372
  679.5 13.4 %collective-permute-start.13 = (bf16[64,64,16]{1,2,0:T(8,128)(2,1)}, bf16[64,64,16]{1,2,0:T(8,128)(2,1)}, u32[]{:S(2)}, u32[]{:S(2)}) collective-permute-start(bf16[64,64,16]{1,2,0:T(8,128)(2,1)} %copy.292), channel_id=1, source_target_pairs={{16,0},{32,16},{48,32},{64,48},{80,64},{96,80},{112,96},{17,1},{33... | collective-permute-start | bytes 393224 | tf_op jit(solution)/shard_map/ppermute | solution.py:18
  680.8 8.8 collective-permute-start.12
  699.2 137.9 %collective-permute-start.15 = (bf16[64,16,160]{2,0,1:T(8,128)(2,1)}, bf16[64,16,160]{2,0,1:T(8,128)(2,1)}, u32[]{:S(2)}, u32[]{:S(2)}) collective-permute-start(bf16[64,16,160]{2,0,1:T(8,128)(2,1)} %get-tuple-element.54), channel_id=1, source_target_pairs={{0,1},{1,2},{2,3},{3,4},{4,5},{5,6},{6,7},{7,8},{8,9},{9,10},{10,1... | collective-permute-start | bytes 983048 | tf_op jit(solution)/shard_map/ppermute | solution.py:15
  703.8 133.3 %collective-permute-start.14 = (bf16[64,16,160]{2,0,1:T(8,128)(2,1)}, bf16[64,16,160]{2,0,1:T(8,128)(2,1)}, u32[]{:S(2)}, u32[]{:S(2)}) collective-permute-start(bf16[64,16,160]{2,0,1:T(8,128)(2,1)} %get-tuple-element.55), channel_id=1, source_target_pairs={{1,0},{2,1},{3,2},{4,3},{5,4},{6,5},{7,6},{8,7},{9,8},{10,9},{11,1... | collective-permute-start | bytes 983048 | tf_op jit(solution)/shard_map/ppermute | solution.py:18
  852.7 31.3 %all-to-all-start.1 = ((f32[1024,1,296]{2,1,0:T(1,128)}), f32[1024,1,296]{2,1,0:T(1,128)}, u32[]{:S(2)}, u32[]{:S(2)}) async-start(f32[1024,1,296]{2,1,0:T(1,128)} %copy.261), calls=%async_computation.1 | async-start | bytes 3145728 | tf_op jit(solution)/shard_map/all_to_all | solution.py:169
  887.0 27.1 %all-to-all-start.2 = ((f32[8,16,8,296]{3,2,0,1:T(8,128)}), f32[8,16,8,296]{3,2,0,1:T(8,128)}, u32[]{:S(2)}, u32[]{:S(2)}) async-start(f32[8,16,8,296]{3,2,0,1:T(8,128)} %copy.263), calls=%async_computation.2 | async-start | bytes 3145728 | tf_op jit(solution)/shard_map/all_to_all | solution.py:176
  926.2 11.2 %copy-start.37 = (f32[5,8,64,128]{3,2,1,0:T(8,128)S(1)}, f32[5,8,64,128]{3,2,1,0:T(8,128)}, u32[]{:S(2)}) copy-start(f32[5,8,64,128]{3,2,1,0:T(8,128)} %copy.361) | copy-start | bytes 3932164
  926.2 12.2 %copy-start.1 = (bf16[37,64]{1,0:T(8,128)(2,1)S(1)}, bf16[37,64]{1,0:T(8,128)(2,1)}, u32[]{:S(2)}) copy-start(bf16[37,64]{1,0:T(8,128)(2,1)} %param.9) | copy-start | bytes 14212
  (40 other events, 132.6 us)
Sparse Core Ops, SparseCore 0:
  686.0 147.6 all-reduce.4
where the time goes:
time: 954 us; the launch traced here: 946 us
  blocking collectives  393 us (41%)
  waiting for transfers between devices  191 us (20%)
  local copies, waits for them, and re-layouts  156 us (16%)
  starting transfers between devices  88.6 us (9%)
  other arithmetic  55 us (6%)
  matrix products  46.3 us (5%)
  between operations  15.3 us (2%)
    psum x2, blocking collectives, normalize(): totals = lax.psum(jnp.sum(activation, axis=(1, 2)), ('row', 'col'))  134 us
    psum x2, blocking collectives, norm_back(): lax.psum((jnp.sum(gradient, axis=(1, 2)), jnp.sum(gradient * normed, axis...  130 us
    psum x2, blocking collectives, normalize(): lax.psum(jnp.sum(centered * centered, axis=(1, 2)), ('row', 'col'))  129 us
    psum x1, waiting for transfers between devices, on_device(): lax.psum((first_term, second_term, head_term, bias_term), ('row', 'col'))  125 us
    unnamed x117, local copies, waits for them, and re-layouts  38.8 us
    ppermute x8, starting transfers between devices, with_halo(): lax.ppermute(lax.slice_in_dim(block, block.shape[dim] - width, None, axis...  31.6 us
    dot_general x36, matrix products, convolve(): jnp.dot(matrix, window, preferred_element_type=jnp.float32)  25.6 us
    convert_element_type x2, local copies, waits for them, and re-layouts, on_device(): cot_mirror.astype(jnp.float32)  23.2 us
  transfers between devices with their start and end apart: 23, of which 9 were waited for; matrix products, arithmetic and copies ran while one was open for 16% of the time, Pallas kernels for 0%

commit v1 on v0

--- a/solution.py
+++ b/solution.py
@@ -5,6 +5,11 @@
 
 DILATION_STEP = 16
 epsilon = 1e-05
+
+
+def summed_here(x, axis):
+    pieces = lax.all_gather(x, axis)
+    return jnp.sum(pieces, axis=0)
 
 
 def with_halo(block, sides, width):
@@ -84,7 +89,7 @@
     totals = lax.psum(jnp.sum(activation, axis=(1, 2)), ("row", "col"))
     average = totals / cell_count
     centered = activation - average[:, None, None]
-    spread = lax.psum(jnp.sum(centered * centered, axis=(1, 2)), ("row", "col")) / cell_count
+    spread = summed_here(jnp.sum(centered * centered, axis=(1, 2)), ("row", "col")) / cell_count
     inverse_std = lax.rsqrt(spread + epsilon)
     return (centered * inverse_std[:, None, None], inverse_std)
 

time: 954 us -> 954 us (level)
    psum x2 -> x0, blocking collectives: 129 us -> none  [normalize(): lax.psum(jnp.sum(centered * centered, axis=(1, 2)), ('row', 'col'))]
    unnamed x0 -> x2, blocking collectives: none -> 129 us
    unnamed x117 -> x121, local copies, waits for them, and re-layouts: 38.8 us -> 39.3 us
where the time goes in v1:
time: 954 us; the launch traced here: 946 us
  blocking collectives  392 us (41%)
  waiting for transfers between devices  191 us (20%)
  local copies, waits for them, and re-layouts  157 us (16%)
  starting transfers between devices  89 us (9%)
  other arithmetic  55.2 us (6%)
  matrix products  46.3 us (5%)
  between operations  15.3 us (2%)
    psum x2, blocking collectives, normalize(): totals = lax.psum(jnp.sum(activation, axis=(1, 2)), ('row', 'col'))  134 us
    psum x2, blocking collectives, norm_back(): lax.psum((jnp.sum(gradient, axis=(1, 2)), jnp.sum(gradient * normed, axis...  129 us
    unnamed x2, blocking collectives  129 us
    psum x1, waiting for transfers between devices, on_device(): lax.psum((first_term, second_term, head_term, bias_term), ('row', 'col'))  125 us
    unnamed x121, local copies, waits for them, and re-layouts  39.3 us
    ppermute x8, starting transfers between devices, with_halo(): lax.ppermute(lax.slice_in_dim(block, block.shape[dim] - width, None, axis...  31.7 us
    dot_general x36, matrix products, convolve(): jnp.dot(matrix, window, preferred_element_type=jnp.float32)  25.6 us
    convert_element_type x2, local copies, waits for them, and re-layouts, on_device(): cot_mirror.astype(jnp.float32)  23.2 us
  transfers between devices with their start and end apart: 23, of which 9 were waited for; matrix products, arithmetic and copies ran while one was open for 16% of the time, Pallas kernels for 0%

profile of v1, /device:TPU:1, one launch (start us, length us, event | category | flops | bytes accessed | tf_op | source)
XLA Modules:
  0.0 945.9 jit_solution(4472165437969287457)
XLA Ops:
  12.6 5.3 collective-permute-start
  21.1 7.8 all-to-all-start.3
  45.4 7.2 collective-permute-done.3
  63.5 67.2 %psum.70 = f32[64]{0:T(128)S(1)} all-reduce(f32[64]{0:T(128)S(1)} %get-tuple-element.108), channel_id=1, replica_groups=mesh['row'=8,'col'=16] {'row','col'}, use_global_device_ids=true, to_apply=%region_1.0 | all-reduce | flops 64 | bytes 512 | tf_op jit(solution)/shard_map/psum | solution.py:89
  131.3 63.5 %all-reduce = f32[8192]{0:T(1024)S(1)} all-reduce(f32[8192]{0:T(1024)S(1)} %dynamic-update-slice), channel_id=2, replica_groups=mesh['row'=8,'col'=16] {'row','col'}, use_global_device_ids=true, to_apply=%add | all-reduce | flops 8192 | bytes 65536
  210.3 4.3 collective-permute-done.5
  233.5 11.3 %all-to-all-start.4 = ((bf16[128,2,1184]{2,1,0:T(2,128)(2,1)}), bf16[128,2,1184]{2,1,0:T(2,128)(2,1)}, u32[]{:S(2)}, u32[]{:S(2)}) async-start(bf16[128,2,1184]{2,1,0:T(2,128)(2,1)} %reshape.303), calls=%async_computation.4 | async-start | bytes 1310720 | tf_op jit(solution)/shard_map/all_to_all | solution.py:141
  247.8 4.2 pad_maximum_fusion.1
  261.2 67.2 %psum.71 = f32[64]{0:T(128)S(1)} all-reduce(f32[64]{0:T(128)S(1)} %get-tuple-element.110), channel_id=1, replica_groups=mesh['row'=8,'col'=16] {'row','col'}, use_global_device_ids=true, to_apply=%region_5.6 | all-reduce | flops 64 | bytes 512 | tf_op jit(solution)/shard_map/psum | solution.py:89
  328.4 6.2 reshape.304
  337.1 4.3 all-to-all-start.5
  343.7 65.1 %all-reduce.1 = f32[8192]{0:T(1024)S(1)} all-reduce(f32[8192]{0:T(1024)S(1)} %dynamic-update-slice.1), channel_id=3, replica_groups=mesh['row'=8,'col'=16] {'row','col'}, use_global_device_ids=true, to_apply=%add.1 | all-reduce | flops 8192 | bytes 65536
  410.2 12.2 %reshape.302 = f32[128,8,37,8]{3,2,1,0:T(8,128)} reshape(f32[16,8,1,8,296]{4,3,1,0,2:T(8,128)} %convert_bitcast_fusion) | data formatting | bytes 2424832 | tf_op jit(solution)/shard_map/convert_element_type | solution.py:216
  422.4 11.1 %copy.273 = f32[37,8,8,128]{3,2,1,0:T(8,128)S(1)} copy(f32[37,8,8,128]{2,0,1,3:T(8,128)} %bitcast.528) | data formatting | bytes 2424832 | tf_op jit(solution)/shard_map/convert_element_type | solution.py:216
  440.3 63.5 %all-reduce.3 = (f32[64]{0:T(128)S(1)}, f32[64]{0:T(128)S(1)}) all-reduce(f32[64]{0:T(128)S(1)} %get-tuple-element.39, f32[64]{0:T(128)S(1)} %get-tuple-element.38), channel_id=1, replica_groups=mesh['row'=8,'col'=16] {'row','col'}, use_global_device_ids=true, to_apply=%region_11.12 | all-reduce | flops 128 | bytes 1024 | tf_op jit(solution)/shard_map/psum | solution.py:98
  525.6 4.7 collective-permute-start.8
  540.1 5.2 copy.259
  548.4 5.6 all-to-all-start
  570.2 8.1 collective-permute-done.11
  578.3 7.2 collective-permute-done.10
  596.7 65.8 %all-reduce.2 = (f32[64]{0:T(128)S(1)}, f32[64]{0:T(128)S(1)}, f32[37,64]{1,0:T(8,128)S(1)}, f32[37]{0:T(128)S(1)}) all-reduce(f32[64]{0:T(128)S(1)} %get-tuple-element.37, f32[64]{0:T(128)S(1)} %get-tuple-element.36, f32[37,64]{1,0:T(8,128)S(1)} %convolution_bitcast_fusion.23, ...), channel_id=1, replica_groups=mesh['row'=8,'col'=16] {'row','col'}, use_global_device_ids=true, to_apply=%region_15.16 | all-reduce | flops 2533 | bytes 20264 | tf_op jit(solution)/shard_map/psum | solution.py:98
  681.1 5.1 collective-permute-start.12
  699.5 4.6 collective-permute-start.15
  708.6 125.4 %all-reduce.7.cloned.1.call-done = (f32[9,64,64]{2,1,0:T(8,128)}, f32[9,64,64]{2,1,0:T(8,128)}) async-done(((f32[9,64,64]{2,1,0:T(8,128)}, f32[9,64,64]{2,1,0:T(8,128)}), (f32[9,64,64]{2,1,0:T(8,128)}, f32[9,64,64]{2,1,0:T(8,128)})) %all-reduce.7.cloned.1.call-update) | async-done | bytes 294928 | tf_op jit(solution)/shard_map/psum | solution.py:243
  837.4 4.9 maximum_maximum_fusion.3
  848.9 4.2 copy.261
  853.1 7.4 all-to-all-start.1
  866.5 17.9 %all-to-all-done.1 = f32[1024,1,296]{2,1,0:T(1,128)} async-done(((f32[1024,1,296]{2,1,0:T(1,128)}), f32[1024,1,296]{2,1,0:T(1,128)}, u32[]{:S(2)}, u32[]{:S(2)}) %all-to-all-start.1) | async-done | bytes 1212448 | tf_op jit(solution)/shard_map/all_to_all | solution.py:174
  887.4 5.5 all-to-all-start.2
  899.0 15.5 %all-to-all-done.2 = f32[8,16,8,296]{3,2,0,1:T(8,128)} async-done(((f32[8,16,8,296]{3,2,0,1:T(8,128)}), f32[8,16,8,296]{3,2,0,1:T(8,128)}, u32[]{:S(2)}, u32[]{:S(2)}) %all-to-all-start.2) | async-done | bytes 1212448 | tf_op jit(solution)/shard_map/all_to_all | solution.py:181
  914.5 12.2 %reshape.301 = f32[128,8,37,8]{3,2,1,0:T(8,128)} reshape(f32[16,8,1,8,296]{4,3,1,0,2:T(8,128)} %bitcast.32) | data formatting | bytes 2424832 | tf_op jit(solution)/shard_map/reshape | solution.py:126
  926.6 11.2 %copy.265 = f32[37,8,8,128]{3,2,1,0:T(8,128)S(1)} copy(f32[37,8,8,128]{2,0,1,3:T(8,128)} %bitcast.529) | data formatting | bytes 2424832 | tf_op jit(solution)/shard_map/transpose | solution.py:126
  (269 shorter events, 219.9 us)
Async XLA Ops:
  7.2 428.6 %copy-start = (bf16[37,64]{1,0:T(8,128)(2,1)S(1)}, bf16[37,64]{1,0:T(8,128)(2,1)}, u32[]{:S(2)}) copy-start(bf16[37,64]{1,0:T(8,128)(2,1)} %param.9) | copy-start | bytes 14212
  10.3 22.1 %collective-permute-start.1 = (bf16[64,64,16]{1,2,0:T(8,128)(2,1)}, bf16[64,64,16]{1,2,0:T(8,128)(2,1)}, u32[]{:S(2)}, u32[]{:S(2)}) collective-permute-start(bf16[64,64,16]{1,2,0:T(8,128)(2,1)} %copy.320), channel_id=1, source_target_pairs={{16,0},{32,16},{48,32},{64,48},{80,64},{96,80},{112,96},{17,1},{33... | collective-permute-start | bytes 393224 | tf_op jit(solution)/shard_map/ppermute | solution.py:23
  12.6 17.0 %collective-permute-start = (bf16[64,64,16]{1,2,0:T(8,128)(2,1)}, bf16[64,64,16]{1,2,0:T(8,128)(2,1)}, u32[]{:S(2)}, u32[]{:S(2)}) collective-permute-start(bf16[64,64,16]{1,2,0:T(8,128)(2,1)} %copy.319), channel_id=1, source_target_pairs={{0,16},{16,32},{32,48},{48,64},{64,80},{80,96},{96,112},{1,17},{17... | collective-permute-start | bytes 393224 | tf_op jit(solution)/shard_map/ppermute | solution.py:20
  21.1 205.4 %all-to-all-start.3 = ((bf16[16,64,296]{2,1,0:T(8,128)(2,1)}), bf16[16,64,296]{2,1,0:T(8,128)(2,1)}, u32[]{:S(2)}, u32[]{:S(2)}) async-start(bf16[16,64,296]{2,1,0:T(8,128)(2,1)} %copy.268), calls=%async_computation.3 | async-start | bytes 1572864 | tf_op jit(solution)/shard_map/all_to_all | solution.py:134
  29.6 23.1 %copy-start.4 = (bf16[64,64,128]{2,0,1:T(8,128)(2,1)}, bf16[64,64,128]{2,0,1:T(8,128)(2,1)S(1)}, u32[]{:S(2)}) copy-start(bf16[64,64,128]{2,0,1:T(8,128)(2,1)S(1)} %copy.226) | copy-start | bytes 3145732
  32.3 20.3 %copy-start.9 = (bf16[64,64,16]{2,0,1:T(8,128)(2,1)}, bf16[64,64,16]{2,0,1:T(8,128)(2,1)S(1)}, u32[]{:S(2)}) copy-start(bf16[64,64,16]{2,0,1:T(8,128)(2,1)S(1)} %copy.225) | copy-start | bytes 393220
  35.1 17.6 %copy-start.7 = (bf16[64,64,16]{2,0,1:T(8,128)(2,1)}, bf16[64,64,16]{2,0,1:T(8,128)(2,1)S(1)}, u32[]{:S(2)}) copy-start(bf16[64,64,16]{2,0,1:T(8,128)(2,1)S(1)} %copy.227) | copy-start | bytes 393220
  35.8 9.7 %collective-permute-start.2 = (bf16[64,16,160]{2,0,1:T(8,128)(2,1)S(1)}, bf16[64,16,160]{2,0,1:T(8,128)(2,1)S(1)}, u32[]{:S(2)}, u32[]{:S(2)}) collective-permute-start(bf16[64,16,160]{2,0,1:T(8,128)(2,1)S(1)} %get-tuple-element.66), channel_id=1, source_target_pairs={{0,1},{1,2},{2,3},{3,4},{4,5},{5,6},{6,7},{7,8},{8,9},{9,10},{10,1... | collective-permute-start | bytes 983048 | tf_op jit(solution)/shard_map/ppermute | solution.py:20
  39.3 13.3 %collective-permute-start.3 = (bf16[64,16,160]{2,0,1:T(8,128)(2,1)S(1)}, bf16[64,16,160]{2,0,1:T(8,128)(2,1)S(1)}, u32[]{:S(2)}, u32[]{:S(2)}) collective-permute-start(bf16[64,16,160]{2,0,1:T(8,128)(2,1)S(1)} %get-tuple-element.67), channel_id=1, source_target_pairs={{1,0},{2,1},{3,2},{4,3},{5,4},{6,5},{7,6},{8,7},{9,8},{10,9},{11,1... | collective-permute-start | bytes 983048 | tf_op jit(solution)/shard_map/ppermute | solution.py:23
  195.6 52.2 %copy-start.2 = (bf16[64,64,128]{2,0,1:T(8,128)(2,1)}, bf16[64,64,128]{2,0,1:T(8,128)(2,1)S(1)}, u32[]{:S(2)}) copy-start(bf16[64,64,128]{2,0,1:T(8,128)(2,1)S(1)} %fusion.5) | copy-start | bytes 3145732
  199.7 7.3 collective-permute-start.4
  205.6 9.0 collective-permute-start.5
  220.7 27.0 %collective-permute-start.7 = (bf16[64,16,160]{2,0,1:T(8,128)(2,1)}, bf16[64,16,160]{2,0,1:T(8,128)(2,1)}, u32[]{:S(2)}, u32[]{:S(2)}) collective-permute-start(bf16[64,16,160]{2,0,1:T(8,128)(2,1)} %get-tuple-element.62), channel_id=1, source_target_pairs={{1,0},{2,1},{3,2},{4,3},{5,4},{6,5},{7,6},{8,7},{9,8},{10,9},{11,1... | collective-permute-start | bytes 983048 | tf_op jit(solution)/shard_map/ppermute | solution.py:23
  224.6 23.2 %collective-permute-start.6 = (bf16[64,16,160]{2,0,1:T(8,128)(2,1)}, bf16[64,16,160]{2,0,1:T(8,128)(2,1)}, u32[]{:S(2)}, u32[]{:S(2)}) collective-permute-start(bf16[64,16,160]{2,0,1:T(8,128)(2,1)} %get-tuple-element.63), channel_id=1, source_target_pairs={{0,1},{1,2},{2,3},{3,4},{4,5},{5,6},{6,7},{7,8},{8,9},{9,10},{10,1... | collective-permute-start | bytes 983048 | tf_op jit(solution)/shard_map/ppermute | solution.py:20
  233.5 94.8 %all-to-all-start.4 = ((bf16[128,2,1184]{2,1,0:T(2,128)(2,1)}), bf16[128,2,1184]{2,1,0:T(2,128)(2,1)}, u32[]{:S(2)}, u32[]{:S(2)}) async-start(bf16[128,2,1184]{2,1,0:T(2,128)(2,1)} %reshape.303), calls=%async_computation.4 | async-start | bytes 1310720 | tf_op jit(solution)/shard_map/all_to_all | solution.py:141
  337.1 71.8 %all-to-all-start.5 = ((bf16[8,16,8,296]{3,2,0,1:T(8,128)(2,1)}), bf16[8,16,8,296]{3,2,0,1:T(8,128)(2,1)S(1)}, u32[]{:S(2)}, u32[]{:S(2)}) async-start(bf16[8,16,8,296]{3,2,0,1:T(8,128)(2,1)} %copy.271), calls=%async_computation.5 | async-start | bytes 1572864 | tf_op jit(solution)/shard_map/all_to_all | solution.py:148
  518.5 11.8 %copy-start.48 = (f32[37]{0:T(128)S(1)}, f32[37]{0:T(128)}, u32[]{:S(2)}) copy-start(f32[37]{0:T(128)} %param.10) | copy-start | bytes 448
  524.3 33.3 %collective-permute-start.9 = (bf16[64,64,16]{1,2,0:T(8,128)(2,1)}, bf16[64,64,16]{1,2,0:T(8,128)(2,1)}, u32[]{:S(2)}, u32[]{:S(2)}) collective-permute-start(bf16[64,64,16]{1,2,0:T(8,128)(2,1)} %copy.276), channel_id=1, source_target_pairs={{16,0},{32,16},{48,32},{64,48},{80,64},{96,80},{112,96},{17,1},{33... | collective-permute-start | bytes 393224 | tf_op jit(solution)/shard_map/ppermute | solution.py:23
  525.6 28.6 %collective-permute-start.8 = (bf16[64,64,16]{1,2,0:T(8,128)(2,1)}, bf16[64,64,16]{1,2,0:T(8,128)(2,1)}, u32[]{:S(2)}, u32[]{:S(2)}) collective-permute-start(bf16[64,64,16]{1,2,0:T(8,128)(2,1)} %copy.275), channel_id=1, source_target_pairs={{0,16},{16,32},{32,48},{48,64},{64,80},{80,96},{96,112},{1,17},{17... | collective-permute-start | bytes 393224 | tf_op jit(solution)/shard_map/ppermute | solution.py:20
  548.4 300.5 %all-to-all-start = ((f32[16,64,296]{2,1,0:T(8,128)}), f32[16,64,296]{2,1,0:T(8,128)}, u32[]{:S(2)}, u32[]{:S(2)}) async-start(f32[16,64,296]{2,1,0:T(8,128)} %copy.260), calls=%async_computation | async-start | bytes 3145728 | tf_op jit(solution)/shard_map/all_to_all | solution.py:167
  554.0 280.0 %all-reduce.7.cloned.1.call-start = ((), (), s32[]{:S(2)}) async-start(), calls=%async_computation.6 | async-start | bytes 1179648 | tf_op jit(solution)/shard_map/psum | solution.py:243
  563.0 15.3 %collective-permute-start.11 = (bf16[64,16,160]{2,0,1:T(8,128)(2,1)S(1)}, bf16[64,16,160]{2,0,1:T(8,128)(2,1)S(1)}, u32[]{:S(2)}, u32[]{:S(2)}) collective-permute-start(bf16[64,16,160]{2,0,1:T(8,128)(2,1)S(1)} %get-tuple-element.58), channel_id=1, source_target_pairs={{0,1},{1,2},{2,3},{3,4},{4,5},{5,6},{6,7},{7,8},{8,9},{9,10},{10,1... | collective-permute-start | bytes 983048 | tf_op jit(solution)/shard_map/ppermute | solution.py:20
  566.5 18.9 %collective-permute-start.10 = (bf16[64,16,160]{2,0,1:T(8,128)(2,1)S(1)}, bf16[64,16,160]{2,0,1:T(8,128)(2,1)S(1)}, u32[]{:S(2)}, u32[]{:S(2)}) collective-permute-start(bf16[64,16,160]{2,0,1:T(8,128)(2,1)S(1)} %get-tuple-element.59), channel_id=1, source_target_pairs={{1,0},{2,1},{3,2},{4,3},{5,4},{6,5},{7,6},{8,7},{9,8},{10,9},{11,1... | collective-permute-start | bytes 983048 | tf_op jit(solution)/shard_map/ppermute | solution.py:23
  673.9 12.3 %copy-start.47 = (f32[9,64,64]{2,1,0:T(8,128)}, f32[9,64,64]{2,1,0:T(8,128)S(1)}, u32[]{:S(2)}) copy-start(f32[9,64,64]{2,1,0:T(8,128)S(1)} %fusion.34) | copy-start | bytes 442372
  679.8 13.4 %collective-permute-start.13 = (bf16[64,64,16]{1,2,0:T(8,128)(2,1)}, bf16[64,64,16]{1,2,0:T(8,128)(2,1)}, u32[]{:S(2)}, u32[]{:S(2)}) collective-permute-start(bf16[64,64,16]{1,2,0:T(8,128)(2,1)} %copy.292), channel_id=1, source_target_pairs={{16,0},{32,16},{48,32},{64,48},{80,64},{96,80},{112,96},{17,1},{33... | collective-permute-start | bytes 393224 | tf_op jit(solution)/shard_map/ppermute | solution.py:23
  681.1 8.8 collective-permute-start.12
  699.5 137.9 %collective-permute-start.15 = (bf16[64,16,160]{2,0,1:T(8,128)(2,1)}, bf16[64,16,160]{2,0,1:T(8,128)(2,1)}, u32[]{:S(2)}, u32[]{:S(2)}) collective-permute-start(bf16[64,16,160]{2,0,1:T(8,128)(2,1)} %get-tuple-element.54), channel_id=1, source_target_pairs={{0,1},{1,2},{2,3},{3,4},{4,5},{5,6},{6,7},{7,8},{8,9},{9,10},{10,1... | collective-permute-start | bytes 983048 | tf_op jit(solution)/shard_map/ppermute | solution.py:20
  704.1 133.3 %collective-permute-start.14 = (bf16[64,16,160]{2,0,1:T(8,128)(2,1)}, bf16[64,16,160]{2,0,1:T(8,128)(2,1)}, u32[]{:S(2)}, u32[]{:S(2)}) collective-permute-start(bf16[64,16,160]{2,0,1:T(8,128)(2,1)} %get-tuple-element.55), channel_id=1, source_target_pairs={{1,0},{2,1},{3,2},{4,3},{5,4},{6,5},{7,6},{8,7},{9,8},{10,9},{11,1... | collective-permute-start | bytes 983048 | tf_op jit(solution)/shard_map/ppermute | solution.py:23
  853.1 31.4 %all-to-all-start.1 = ((f32[1024,1,296]{2,1,0:T(1,128)}), f32[1024,1,296]{2,1,0:T(1,128)}, u32[]{:S(2)}, u32[]{:S(2)}) async-start(f32[1024,1,296]{2,1,0:T(1,128)} %copy.261), calls=%async_computation.1 | async-start | bytes 3145728 | tf_op jit(solution)/shard_map/all_to_all | solution.py:174
  887.4 27.1 %all-to-all-start.2 = ((f32[8,16,8,296]{3,2,0,1:T(8,128)}), f32[8,16,8,296]{3,2,0,1:T(8,128)}, u32[]{:S(2)}, u32[]{:S(2)}) async-start(f32[8,16,8,296]{3,2,0,1:T(8,128)} %copy.263), calls=%async_computation.2 | async-start | bytes 3145728 | tf_op jit(solution)/shard_map/all_to_all | solution.py:181
  926.6 11.2 %copy-start.37 = (f32[5,8,64,128]{3,2,1,0:T(8,128)S(1)}, f32[5,8,64,128]{3,2,1,0:T(8,128)}, u32[]{:S(2)}) copy-start(f32[5,8,64,128]{3,2,1,0:T(8,128)} %copy.361) | copy-start | bytes 3932164
  926.6 12.2 %copy-start.1 = (bf16[37,64]{1,0:T(8,128)(2,1)S(1)}, bf16[37,64]{1,0:T(8,128)(2,1)}, u32[]{:S(2)}) copy-start(bf16[37,64]{1,0:T(8,128)(2,1)} %param.9) | copy-start | bytes 14212
  (40 other events, 132.6 us)
Sparse Core Ops, SparseCore 0:
  686.4 147.6 all-reduce.6
